TPU v7x, 512 devices: a whole 4x4x16 slice. The times are simulated.
512 devices in a mesh: group: 16 (over y, z_hi), seq: 32 (over x, z_lo, core).
Axes of the slice: x: 4, y: 4, z: 16 (z_hi: 4, z_lo: 4; z = z_hi * 4 + z_lo), core: 2. Of those that a mesh axis runs over, the one named last changes fastest.
Arguments:
- features: bfloat16 [65536, 768], P(('group', 'seq')), may hold values from -6 to 6
- tiles: bfloat16 [65536, 1024], P(('group', 'seq')), may hold values from -0.5 to 0.5
- tile_src: int32 [512, 8], P(('group', 'seq')), may hold values from 0 to 15
- tile_count: int32 [512], P(('group', 'seq')), may hold values from 1 to 8, as said below
- node_bucket: int32 [65536], P(('group', 'seq')), may hold values from 0 to 15
- w_qk: bfloat16 [768, 1536], replicated, may hold values from -0.3125 to 0.3125
- w_v: bfloat16 [768, 768], replicated, may hold values from -1.25 to 1.25
- bias_table: float32 [32, 256], replicated, may hold values from -2 to 300
Outputs:
- attended: bfloat16 [65536, 768], P(('group', 'seq'))
Inputs may be any that keep to these rules, and one draw needn't show every extreme that they name: `tile_count`: some row block uses all 8 slots.
All inputs are finite; a program needn't handle non-finite values.
Results may differ from a plain program's by a relative error of at most 0.012.
Values may be sent and summed in bfloat16 or wider, within the bound.
A program may use at most 64 MiB of HBM per device.

v0:
```python
import math
import jax
import jax.numpy as jnp
from jax import lax
from jax.sharding import PartitionSpec as P

H = 32
HD = 24
NB = 16
TILES = 8


def on_device(features, tiles, tile_src, tile_count, node_bucket, w_qk, w_v, bias_table):
    row_count, feat_width = features.shape
    group_count = lax.axis_size("group")
    live_flag = jnp.arange(TILES) < tile_count[0]
    tile_rows = tiles.reshape(row_count, TILES, row_count)
    sources = tile_src[0]
    gathered = lax.all_gather(features, "group", axis=0, tiled=True)
    chosen = gathered.reshape(group_count, row_count, feat_width)[sources]
    masked = tile_rows * live_flag.astype(jnp.bfloat16)[None, :, None]
    aggregated = features.astype(jnp.float32) + jnp.einsum(
        "rtc,tcd->rd", masked, chosen, preferred_element_type=jnp.float32
    )
    mean_square = jnp.mean(aggregated * aggregated, axis=-1, keepdims=True)
    normed = (aggregated * lax.rsqrt(mean_square + 1e-06)).astype(jnp.bfloat16)
    query_key = jnp.dot(normed, w_qk, preferred_element_type=jnp.float32).astype(jnp.bfloat16)
    values = jnp.dot(normed, w_v, preferred_element_type=jnp.float32).astype(jnp.bfloat16)
    bias_cube = bias_table.reshape(H, NB, NB)
    scale = 1.0 / math.sqrt(HD)
    iota_nb = jnp.arange(NB)
    queries = query_key[:, :feat_width].reshape(row_count, H, HD)
    keys_own = query_key[:, feat_width:]
    query_bias = bias_cube[:, node_bucket, :]
    start_state = (
        jnp.full((H, row_count), -1e30, jnp.float32),
        jnp.zeros((H, row_count), jnp.float32),
        jnp.zeros((H, row_count, HD), jnp.float32),
    )
    key_rows = lax.all_gather(keys_own, "seq", axis=0, tiled=True)
    value_rows = lax.all_gather(values, "seq", axis=0, tiled=True)
    bucket_rows = lax.all_gather(node_bucket, "seq", axis=0, tiled=True)
    key_total = key_rows.shape[0]
    key_block = math.gcd(key_total, 512)

    def one_block(block_index, state_in):
        peak_old, total_old, accum_old = state_in
        offset = block_index * key_block
        key_part = lax.dynamic_slice_in_dim(key_rows, offset, key_block, 0).reshape(
            key_block, H, HD
        )
        value_part = lax.dynamic_slice_in_dim(value_rows, offset, key_block, 0).reshape(
            key_block, H, HD
        )
        bucket_part = lax.dynamic_slice_in_dim(bucket_rows, offset, key_block, 0)
        onehot = (bucket_part[:, None] == iota_nb[None, :]).astype(jnp.float32)
        scores = (
            jnp.einsum("rhd,nhd->hrn", queries, key_part, preferred_element_type=jnp.float32)
            * scale
        )
        scores = scores + jnp.einsum(
            "hrb,nb->hrn", query_bias, onehot, precision=lax.Precision.HIGHEST
        )
        peak_new = jnp.maximum(peak_old, jnp.max(scores, axis=-1))
        factor = jnp.exp(peak_old - peak_new)
        weights = jnp.exp(scores - peak_new[..., None])
        total_new = total_old * factor + jnp.sum(weights, axis=-1)
        accum_new = accum_old * factor[..., None] + jnp.einsum(
            "hrn,nhd->hrd",
            weights.astype(jnp.bfloat16),
            value_part,
            preferred_element_type=jnp.float32,
        )
        return (peak_new, total_new, accum_new)

    peak_end, total_end, accum_end = lax.fori_loop(
        0, key_total // key_block, one_block, start_state
    )
    heads_out = accum_end / total_end[..., None]
    attended = heads_out.transpose(1, 0, 2).reshape(row_count, feat_width).astype(jnp.bfloat16)
    return attended


def solution(mesh):
    in_specs = (
        P(("group", "seq"), None),
        P(("group", "seq"), None),
        P(("group", "seq"), None),
        P(("group", "seq")),
        P(("group", "seq")),
        P(),
        P(),
        P(),
    )
    out_specs = P(("group", "seq"), None)
    return jax.shard_map(
        on_device, mesh=mesh, in_specs=in_specs, out_specs=out_specs, check_vma=False
    )
```

profile of v0, /device:TPU:1, one launch (start us, length us, event | category | flops | bytes accessed | tf_op | source)
XLA Modules:
  0.0 412.8 jit_solution(12334973029780764622)
XLA Ops:
  8.6 121.5 %all-gather.5.cloned.1.call-done = bf16[2048,768]{1,0:T(8,128)(2,1)} async-done(((bf16[128,768]{1,0:T(8,128)(2,1)}), bf16[2048,768]{1,0:T(8,128)(2,1)}) %all-gather.5.cloned.1.call-update) | async-done | bytes 3145744 | tf_op jit(solution)/shard_map/all_gather | solution.py:19
  130.1 3.7 gather_fusion
  133.8 2.0 multiply_reduce_fusion
  137.1 2.3 convolution_convert_fusion.1
  139.6 1.8 gather_fusion.1
  141.4 2.4 copy.28
  143.7 39.3 %all-gather = s32[32,1,128]{2,1,0:T(1,128)S(1)} all-gather(s32[1,1,128]{2,1,0:T(1,128)S(1)} %bitcast.66), channel_id=1, replica_groups=mesh['group'=16,'seq'=32] {'seq'}, dimensions={0}, use_global_device_ids=true | all-gather | bytes 16896 | tf_op jit(solution)/shard_map/all_gather | solution.py:42
  183.9 19.7 %all-gather.7.cloned.1.call-done = bf16[4096,768]{1,0:T(8,128)(2,1)} async-done(((bf16[128,768]{1,0:T(8,128)(2,1)}), bf16[4096,768]{1,0:T(8,128)(2,1)}) %all-gather.7.cloned.1.call-update) | async-done | bytes 6291472 | tf_op jit(solution)/shard_map/all_gather | solution.py:40
  203.6 71.9 %all-gather.9.cloned.1.call-done = bf16[4096,768]{1,0:T(8,128)(2,1)} async-done(((bf16[128,768]{1,0:T(8,128)(2,1)}), bf16[4096,768]{1,0:T(8,128)(2,1)}) %all-gather.9.cloned.1.call-update) | async-done | bytes 6291472 | tf_op jit(solution)/shard_map/all_gather | solution.py:41
  275.5 129.1 %while.18 = (s32[]{:T(128)}, f32[32,128]{1,0:T(8,128)S(1)}, f32[32,128]{1,0:T(8,128)}, f32[32,128,24]{1,2,0:T(8,128)S(1)}, bf16[4096,768]{1,0:T(8,128)(2,1)}, /*...) while((s32[]{:T(128)}, f32[32,128]{1,0:T(8,128)S(1)}, ...), condition=%wide.region_4.0_spmd.clone, body=%wide.region_1.0_spmd.clone.sunk | while | flops 618983424 | bytes 55515500 | solution.py:76
  276.2 2.7 constant_dynamic-slice_fusion.3
  278.9 1.4 copy.43
  280.3 2.4 copy.44
  282.7 4.5 %fusion.46 = f32[512,32,128]{2,0,1:T(8,128)S(1)} fusion(f32[32,128,16]{1,2,0:T(8,128)} %get-tuple-element.364, s32[512]{0:T(512)} %dynamic_slice.29), kind=kOutput, calls=%fused_computation.13.clone.1 | convolution fusion | flops 402661376 | bytes 8652800 | tf_op jit(solution)/shard_map/while/body/eval_jaxpr/hrb,nb->hrn/dot_general | solution.py:61
  287.2 1.8 fusion.47
  289.1 1.3 fusion.48
  290.4 1.2 fusion.50
  292.4 2.7 constant_dynamic-slice_fusion.3
  295.0 1.4 copy.43
  296.4 2.4 copy.44
  298.8 4.5 %fusion.46 = f32[512,32,128]{2,0,1:T(8,128)S(1)} fusion(f32[32,128,16]{1,2,0:T(8,128)} %get-tuple-element.364, s32[512]{0:T(512)} %dynamic_slice.29), kind=kOutput, calls=%fused_computation.13.clone.1 | convolution fusion | flops 402661376 | bytes 8652800 | tf_op jit(solution)/shard_map/while/body/eval_jaxpr/hrb,nb->hrn/dot_general | solution.py:61
  303.3 1.8 fusion.47
  305.2 1.3 fusion.48
  306.5 1.2 fusion.50
  308.5 2.7 constant_dynamic-slice_fusion.3
  311.2 1.4 copy.43
  312.6 2.4 copy.44
  314.9 4.5 %fusion.46 = f32[512,32,128]{2,0,1:T(8,128)S(1)} fusion(f32[32,128,16]{1,2,0:T(8,128)} %get-tuple-element.364, s32[512]{0:T(512)} %dynamic_slice.29), kind=kOutput, calls=%fused_computation.13.clone.1 | convolution fusion | flops 402661376 | bytes 8652800 | tf_op jit(solution)/shard_map/while/body/eval_jaxpr/hrb,nb->hrn/dot_general | solution.py:61
  319.5 1.8 fusion.47
  321.4 1.3 fusion.48
  322.7 1.2 fusion.50
  324.6 2.7 constant_dynamic-slice_fusion.3
  327.3 1.4 copy.43
  328.7 2.4 copy.44
  331.1 4.5 %fusion.46 = f32[512,32,128]{2,0,1:T(8,128)S(1)} fusion(f32[32,128,16]{1,2,0:T(8,128)} %get-tuple-element.364, s32[512]{0:T(512)} %dynamic_slice.29), kind=kOutput, calls=%fused_computation.13.clone.1 | convolution fusion | flops 402661376 | bytes 8652800 | tf_op jit(solution)/shard_map/while/body/eval_jaxpr/hrb,nb->hrn/dot_general | solution.py:61
  335.6 1.8 fusion.47
  337.5 1.3 fusion.48
  340.8 2.7 constant_dynamic-slice_fusion.3
  343.4 1.4 copy.43
  344.9 2.4 copy.44
  347.2 4.5 %fusion.46 = f32[512,32,128]{2,0,1:T(8,128)S(1)} fusion(f32[32,128,16]{1,2,0:T(8,128)} %get-tuple-element.364, s32[512]{0:T(512)} %dynamic_slice.29), kind=kOutput, calls=%fused_computation.13.clone.1 | convolution fusion | flops 402661376 | bytes 8652800 | tf_op jit(solution)/shard_map/while/body/eval_jaxpr/hrb,nb->hrn/dot_general | solution.py:61
  351.8 1.8 fusion.47
  353.6 1.3 fusion.48
  356.9 2.7 constant_dynamic-slice_fusion.3
  359.6 1.4 copy.43
  361.0 2.4 copy.44
  363.4 4.5 %fusion.46 = f32[512,32,128]{2,0,1:T(8,128)S(1)} fusion(f32[32,128,16]{1,2,0:T(8,128)} %get-tuple-element.364, s32[512]{0:T(512)} %dynamic_slice.29), kind=kOutput, calls=%fused_computation.13.clone.1 | convolution fusion | flops 402661376 | bytes 8652800 | tf_op jit(solution)/shard_map/while/body/eval_jaxpr/hrb,nb->hrn/dot_general | solution.py:61
  367.9 1.8 fusion.47
  369.8 1.3 fusion.48
  371.1 1.2 fusion.50
  373.1 2.7 constant_dynamic-slice_fusion.3
  375.7 1.4 copy.43
  377.1 2.4 copy.44
  379.5 4.5 %fusion.46 = f32[512,32,128]{2,0,1:T(8,128)S(1)} fusion(f32[32,128,16]{1,2,0:T(8,128)} %get-tuple-element.364, s32[512]{0:T(512)} %dynamic_slice.29), kind=kOutput, calls=%fused_computation.13.clone.1 | convolution fusion | flops 402661376 | bytes 8652800 | tf_op jit(solution)/shard_map/while/body/eval_jaxpr/hrb,nb->hrn/dot_general | solution.py:61
  384.0 1.8 fusion.47
  385.9 1.3 fusion.48
  387.3 1.2 fusion.50
  389.2 2.7 constant_dynamic-slice_fusion.3
  391.9 1.4 copy.43
  393.3 2.4 copy.44
  395.7 4.5 %fusion.46 = f32[512,32,128]{2,0,1:T(8,128)S(1)} fusion(f32[32,128,16]{1,2,0:T(8,128)} %get-tuple-element.364, s32[512]{0:T(512)} %dynamic_slice.29), kind=kOutput, calls=%fused_computation.13.clone.1 | convolution fusion | flops 402661376 | bytes 8652800 | tf_op jit(solution)/shard_map/while/body/eval_jaxpr/hrb,nb->hrn/dot_general | solution.py:61
  400.2 1.8 fusion.47
  402.1 1.3 fusion.48
  403.4 1.2 fusion.50
  (157 shorter events, 13.4 us)
Async XLA Ops:
  6.5 129.2 %copy-start = (bf16[768,1536]{1,0:T(8,128)(2,1)S(1)}, bf16[768,1536]{1,0:T(8,128)(2,1)}, u32[]{:S(2)}) copy-start(bf16[768,1536]{1,0:T(8,128)(2,1)} %param.15) | copy-start | bytes 7077892
  6.5 132.9 %copy-start.7 = (f32[32,256]{1,0:T(8,128)S(1)}, f32[32,256]{1,0:T(8,128)}, u32[]{:S(2)}) copy-start(f32[32,256]{1,0:T(8,128)} %param.17) | copy-start | bytes 98308
  6.5 133.0 %copy-start.8 = (s32[128]{0:T(128)S(1)}, s32[128]{0:T(128)}, u32[]{:S(2)}) copy-start(s32[128]{0:T(128)} %param.14) | copy-start | bytes 1540
  6.5 123.5 %all-gather.5.cloned.1.call-start = ((), (), s32[]{:S(2)}) async-start(), calls=%async_computation | async-start | bytes 3342336 | tf_op jit(solution)/shard_map/all_gather | solution.py:19
  7.3 196.3 %all-gather.7.cloned.1.call-start = ((), (), s32[]{:S(2)}) async-start(), calls=%async_computation.1 | async-start | bytes 6488064 | tf_op jit(solution)/shard_map/all_gather | solution.py:40
  137.0 138.5 %all-gather.9.cloned.1.call-start = ((), (), s32[]{:S(2)}) async-start(), calls=%async_computation.2 | async-start | bytes 6488064 | tf_op jit(solution)/shard_map/all_gather | solution.py:41
  275.5 3.3 copy-start.5
  282.7 4.5 %copy-start.2 = (bf16[128,32,24]{0,2,1:T(8,128)(2,1)S(1)}, bf16[128,32,24]{0,2,1:T(8,128)(2,1)}, u32[]{:S(2)}) copy-start(bf16[128,32,24]{0,2,1:T(8,128)(2,1)} %get-tuple-element.362) | copy-start | bytes 589828 | tf_op jit(solution)/shard_map/while
  289.0 1.3 copy-start.3
  289.0 1.3 copy-start.1
  290.4 1.3 copy-start.6
  290.4 1.3 copy-start.4
  291.7 3.4 copy-start.5
  298.8 4.5 %copy-start.2 = (bf16[128,32,24]{0,2,1:T(8,128)(2,1)S(1)}, bf16[128,32,24]{0,2,1:T(8,128)(2,1)}, u32[]{:S(2)}) copy-start(bf16[128,32,24]{0,2,1:T(8,128)(2,1)} %get-tuple-element.362) | copy-start | bytes 589828 | tf_op jit(solution)/shard_map/while
  305.2 1.3 copy-start.3
  305.2 1.3 copy-start.1
  306.5 1.3 copy-start.6
  306.5 1.3 copy-start.4
  307.8 3.4 copy-start.5
  314.9 4.5 %copy-start.2 = (bf16[128,32,24]{0,2,1:T(8,128)(2,1)S(1)}, bf16[128,32,24]{0,2,1:T(8,128)(2,1)}, u32[]{:S(2)}) copy-start(bf16[128,32,24]{0,2,1:T(8,128)(2,1)} %get-tuple-element.362) | copy-start | bytes 589828 | tf_op jit(solution)/shard_map/while
  321.3 1.3 copy-start.3
  321.3 1.3 copy-start.1
  322.6 1.3 copy-start.6
  322.7 1.3 copy-start.4
  324.0 3.4 copy-start.5
  331.1 4.5 %copy-start.2 = (bf16[128,32,24]{0,2,1:T(8,128)(2,1)S(1)}, bf16[128,32,24]{0,2,1:T(8,128)(2,1)}, u32[]{:S(2)}) copy-start(bf16[128,32,24]{0,2,1:T(8,128)(2,1)} %get-tuple-element.362) | copy-start | bytes 589828 | tf_op jit(solution)/shard_map/while
  337.5 1.3 copy-start.3
  337.5 1.3 copy-start.1
  338.8 1.3 copy-start.6
  338.8 1.3 copy-start.4
  340.1 3.4 copy-start.5
  347.2 4.5 %copy-start.2 = (bf16[128,32,24]{0,2,1:T(8,128)(2,1)S(1)}, bf16[128,32,24]{0,2,1:T(8,128)(2,1)}, u32[]{:S(2)}) copy-start(bf16[128,32,24]{0,2,1:T(8,128)(2,1)} %get-tuple-element.362) | copy-start | bytes 589828 | tf_op jit(solution)/shard_map/while
  353.6 1.3 copy-start.3
  353.6 1.3 copy-start.1
  354.9 1.3 copy-start.6
  355.0 1.3 copy-start.4
  356.2 3.4 copy-start.5
  363.4 4.5 %copy-start.2 = (bf16[128,32,24]{0,2,1:T(8,128)(2,1)S(1)}, bf16[128,32,24]{0,2,1:T(8,128)(2,1)}, u32[]{:S(2)}) copy-start(bf16[128,32,24]{0,2,1:T(8,128)(2,1)} %get-tuple-element.362) | copy-start | bytes 589828 | tf_op jit(solution)/shard_map/while
  369.8 1.3 copy-start.3
  369.8 1.3 copy-start.1
  371.1 1.3 copy-start.6
  371.1 1.3 copy-start.4
  372.4 3.4 copy-start.5
  379.5 4.5 %copy-start.2 = (bf16[128,32,24]{0,2,1:T(8,128)(2,1)S(1)}, bf16[128,32,24]{0,2,1:T(8,128)(2,1)}, u32[]{:S(2)}) copy-start(bf16[128,32,24]{0,2,1:T(8,128)(2,1)} %get-tuple-element.362) | copy-start | bytes 589828 | tf_op jit(solution)/shard_map/while
  385.9 1.3 copy-start.3
  385.9 1.3 copy-start.1
  387.2 1.3 copy-start.6
  387.2 1.3 copy-start.4
  388.5 3.4 copy-start.5
  395.7 4.5 %copy-start.2 = (bf16[128,32,24]{0,2,1:T(8,128)(2,1)S(1)}, bf16[128,32,24]{0,2,1:T(8,128)(2,1)}, u32[]{:S(2)}) copy-start(bf16[128,32,24]{0,2,1:T(8,128)(2,1)} %get-tuple-element.362) | copy-start | bytes 589828 | tf_op jit(solution)/shard_map/while
  402.0 1.3 copy-start.3
  402.0 1.3 copy-start.1
  403.3 1.3 copy-start.6
  403.4 1.3 copy-start.4
Sparse Core Ops, SparseCore 0:
  10.4 119.6 all-gather.4
  137.1 66.4 all-gather.6
  205.8 69.7 all-gather.8
where the time goes:
time: 414 us; the launch traced here: 413 us
  waiting for transfers between devices  214 us (52%)
  local copies, waits for them, and re-layouts  67.4 us (16%)
  matrix products  65.4 us (16%)
  blocking collectives  39.3 us (9%)
  between operations  13.9 us (3%)
  other arithmetic  11.7 us (3%)
    all_gather x1, waiting for transfers between devices, on_device(): gathered = lax.all_gather(features, 'group', axis=0, tiled=True)  121 us
    all_gather x1, waiting for transfers between devices, on_device(): value_rows = lax.all_gather(values, 'seq', axis=0, tiled=True)  71.9 us
    dynamic_slice x16, local copies, waits for them, and re-layouts, one_block(): lax.dynamic_slice_in_dim(value_rows, offset, key_block, 0)  40.3 us
    all_gather x1, blocking collectives, on_device(): bucket_rows = lax.all_gather(node_bucket, 'seq', axis=0, tiled=True)  39.3 us
    dot_general x8, matrix products, one_block(): jnp.einsum('hrb,nb->hrn', query_bias, onehot, precision=lax.Precision.HIG...  36.1 us
    all_gather x1, waiting for transfers between devices, on_device(): key_rows = lax.all_gather(keys_own, 'seq', axis=0, tiled=True)  19.7 us
    dot_general x8, matrix products, one_block(): jnp.einsum('rhd,nhd->hrn', queries, key_part, preferred_element_type=jnp....  14.7 us
    dynamic_slice x8, local copies, waits for them, and re-layouts, one_block(): lax.dynamic_slice_in_dim(key_rows, offset, key_block, 0)  11.3 us
  transfers between devices with their start and end apart: 3, of which 3 were waited for; matrix products, arithmetic and copies ran while one was open for 2% of the time, Pallas kernels for 0%

commit v1 on v0

--- a/solution.py
+++ b/solution.py
@@ -11,12 +11,22 @@
 
 
 def on_device(features, tiles, tile_src, tile_count, node_bucket, w_qk, w_v, bias_table):
+
+    def refer_corner(block_in, in_dim):
+        later = jnp.concatenate(
+            lax.all_to_all(
+                jnp.stack(tuple((block_in for _ in range(lax.axis_size("group"))))), "group", 0, 0
+            ),
+            axis=in_dim,
+        )
+        return later
+
     row_count, feat_width = features.shape
     group_count = lax.axis_size("group")
     live_flag = jnp.arange(TILES) < tile_count[0]
     tile_rows = tiles.reshape(row_count, TILES, row_count)
     sources = tile_src[0]
-    gathered = lax.all_gather(features, "group", axis=0, tiled=True)
+    gathered = refer_corner(features, 0)
     chosen = gathered.reshape(group_count, row_count, feat_width)[sources]
     masked = tile_rows * live_flag.astype(jnp.bfloat16)[None, :, None]
     aggregated = features.astype(jnp.float32) + jnp.einsum(

time: 414 us -> 457 us (1.10)
  starting transfers between devices: 0.08 us -> 18.6 us
  waiting for transfers between devices: 214 us -> 230 us
  blocking collectives: 39.3 us -> 44.7 us
    all_to_all x0 -> x1, waiting for transfers between devices: none -> 140 us  [refer_corner(): lax.all_to_all(jnp.stack(tuple((block_in for _ in range(lax.axis_size('gr...]
    all_gather x1 -> x0, waiting for transfers between devices: 121 us -> none  [on_device(): gathered = lax.all_gather(features, 'group', axis=0, tiled=True)]
    all_to_all x0 -> x1, starting transfers between devices: none -> 18.5 us  [refer_corner(): lax.all_to_all(jnp.stack(tuple((block_in for _ in range(lax.axis_size('gr...]
    all_gather x1, blocking collectives: 39.3 us -> 44.7 us  [on_device(): bucket_rows = lax.all_gather(node_bucket, 'seq', axis=0, tiled=True)]
where the time goes in v1:
time: 457 us; the launch traced here: 456 us
  waiting for transfers between devices  230 us (50%)
  local copies, waits for them, and re-layouts  70.4 us (15%)
  matrix products  65.3 us (14%)
  blocking collectives  44.7 us (10%)
  starting transfers between devices  18.6 us (4%)
  between operations  14.2 us (3%)
  other arithmetic  11 us (2%)
    all_to_all x1, waiting for transfers between devices, refer_corner(): lax.all_to_all(jnp.stack(tuple((block_in for _ in range(lax.axis_size('gr...  140 us
    all_gather x1, waiting for transfers between devices, on_device(): value_rows = lax.all_gather(values, 'seq', axis=0, tiled=True)  71.8 us
    all_gather x1, blocking collectives, on_device(): bucket_rows = lax.all_gather(node_bucket, 'seq', axis=0, tiled=True)  44.7 us
    dynamic_slice x16, local copies, waits for them, and re-layouts, one_block(): lax.dynamic_slice_in_dim(value_rows, offset, key_block, 0)  40.1 us
    dot_general x8, matrix products, one_block(): jnp.einsum('hrb,nb->hrn', query_bias, onehot, precision=lax.Precision.HIG...  36.1 us
    all_to_all x1, starting transfers between devices, refer_corner(): lax.all_to_all(jnp.stack(tuple((block_in for _ in range(lax.axis_size('gr...  18.5 us
    all_gather x1, waiting for transfers between devices, on_device(): key_rows = lax.all_gather(keys_own, 'seq', axis=0, tiled=True)  18.3 us
    dot_general x8, matrix products, one_block(): jnp.einsum('rhd,nhd->hrn', queries, key_part, preferred_element_type=jnp....  14.7 us
  transfers between devices with their start and end apart: 3, of which 3 were waited for; matrix products, arithmetic and copies ran while one was open for 2% of the time, Pallas kernels for 0%

profile of v1, /device:TPU:1, one launch (start us, length us, event | category | flops | bytes accessed | tf_op | source)
XLA Modules:
  0.0 455.7 jit_solution(7229768738576481999)
XLA Ops:
  6.5 3.1 stack.2
  9.6 18.5 %all-to-all-start = ((bf16[16,128,768]{2,1,0:T(8,128)(2,1)}), bf16[16,128,768]{2,1,0:T(8,128)(2,1)}, u32[]{:S(2)}, u32[]{:S(2)}) async-start(bf16[16,128,768]{2,1,0:T(8,128)(2,1)} %stack.2), calls=%async_computation | async-start | bytes 6291456 | tf_op jit(solution)/shard_map/all_to_all | solution.py:17
  28.9 140.3 %all-to-all-done = bf16[16,128,768]{2,1,0:T(8,128)(2,1)} async-done(((bf16[16,128,768]{2,1,0:T(8,128)(2,1)}), bf16[16,128,768]{2,1,0:T(8,128)(2,1)}, u32[]{:S(2)}, u32[]{:S(2)}) %all-to-all-start) | async-done | bytes 3145760 | tf_op jit(solution)/shard_map/all_to_all | solution.py:17
  169.2 3.7 gather_fusion
  172.9 1.9 multiply_reduce_fusion
  176.1 2.3 convolution_convert_fusion.1
  178.6 1.8 gather_fusion.1
  180.4 2.4 copy.28
  182.8 44.7 %all-gather = s32[32,1,128]{2,1,0:T(1,128)S(1)} all-gather(s32[1,1,128]{2,1,0:T(1,128)S(1)} %bitcast.64), channel_id=1, replica_groups=mesh['group'=16,'seq'=32] {'seq'}, dimensions={0}, use_global_device_ids=true | all-gather | bytes 16896 | tf_op jit(solution)/shard_map/all_gather | solution.py:52
  228.3 18.3 %all-gather.4.cloned.1.call-done = bf16[4096,768]{1,0:T(8,128)(2,1)} async-done(((bf16[128,768]{1,0:T(8,128)(2,1)}), bf16[4096,768]{1,0:T(8,128)(2,1)}) %all-gather.4.cloned.1.call-update) | async-done | bytes 6291472 | tf_op jit(solution)/shard_map/all_gather | solution.py:50
  246.6 71.8 %all-gather.6.cloned.1.call-done = bf16[4096,768]{1,0:T(8,128)(2,1)} async-done(((bf16[128,768]{1,0:T(8,128)(2,1)}), bf16[4096,768]{1,0:T(8,128)(2,1)}) %all-gather.6.cloned.1.call-update) | async-done | bytes 6291472 | tf_op jit(solution)/shard_map/all_gather | solution.py:51
  318.3 129.0 %while.18 = (s32[]{:T(128)}, f32[32,128]{1,0:T(8,128)S(1)}, f32[32,128]{1,0:T(8,128)}, f32[32,128,24]{1,2,0:T(8,128)S(1)}, bf16[4096,768]{1,0:T(8,128)(2,1)}, /*...) while((s32[]{:T(128)}, f32[32,128]{1,0:T(8,128)S(1)}, ...), condition=%wide.region_4.0_spmd.clone, body=%wide.region_1.0_spmd.clone.sunk | while | flops 618983424 | bytes 55515500 | solution.py:86
  319.0 2.7 constant_dynamic-slice_fusion.3
  321.6 1.4 copy.43
  323.0 2.4 copy.44
  325.4 4.5 fusion.46
  329.9 1.8 fusion.47
  331.8 1.3 fusion.48
  333.1 1.2 fusion.50
  335.1 2.7 constant_dynamic-slice_fusion.3
  337.8 1.4 copy.43
  339.2 2.4 copy.44
  341.5 4.5 fusion.46
  346.1 1.8 fusion.47
  347.9 1.3 fusion.48
  351.2 2.7 constant_dynamic-slice_fusion.3
  353.9 1.4 copy.43
  355.3 2.4 copy.44
  357.7 4.5 fusion.46
  362.2 1.8 fusion.47
  364.1 1.3 fusion.48
  367.4 2.7 constant_dynamic-slice_fusion.3
  370.0 1.4 copy.43
  371.4 2.4 copy.44
  373.8 4.5 fusion.46
  378.3 1.8 fusion.47
  380.2 1.3 fusion.48
  381.5 1.2 fusion.50
  383.5 2.7 constant_dynamic-slice_fusion.3
  386.1 1.4 copy.43
  387.5 2.4 copy.44
  389.9 4.5 fusion.46
  394.4 1.8 fusion.47
  396.3 1.3 fusion.48
  399.6 2.7 constant_dynamic-slice_fusion.3
  402.3 1.4 copy.43
  403.7 2.4 copy.44
  406.0 4.5 fusion.46
  410.6 1.8 fusion.47
  412.4 1.3 fusion.48
  415.7 2.7 constant_dynamic-slice_fusion.3
  418.4 1.4 copy.43
  419.8 2.4 copy.44
  422.2 4.5 fusion.46
  426.7 1.8 fusion.47
  428.6 1.3 fusion.48
  429.9 1.2 fusion.50
  431.8 2.7 constant_dynamic-slice_fusion.3
  434.5 1.4 copy.43
  435.9 2.4 copy.44
  438.3 4.5 fusion.46
  442.8 1.8 fusion.47
  444.7 1.3 fusion.48
  446.0 1.2 fusion.50
  (163 shorter events, 14.5 us)
Async XLA Ops:
  6.5 168.3 %copy-start = (bf16[768,1536]{1,0:T(8,128)(2,1)S(1)}, bf16[768,1536]{1,0:T(8,128)(2,1)}, u32[]{:S(2)}) copy-start(bf16[768,1536]{1,0:T(8,128)(2,1)} %param.15) | copy-start | bytes 7077892
  6.5 22.3 %copy-start.11 = (s32[1,8]{1,0:T(1,128)S(1)}, s32[1,8]{1,0:T(1,128)}, u32[]{:S(2)}) copy-start(s32[1,8]{1,0:T(1,128)} %param.12) | copy-start | bytes 100
  9.6 163.3 %copy-start.3 = (bf16[128,768]{1,0:T(8,128)(2,1)S(1)}, bf16[128,768]{1,0:T(8,128)(2,1)}, u32[]{:S(2)}) copy-start(bf16[128,768]{1,0:T(8,128)(2,1)} %param.10) | copy-start | bytes 589828
  9.6 163.3 %copy-start.6 = (bf16[128,1024]{1,0:T(8,128)(2,1)S(1)}, bf16[128,1024]{1,0:T(8,128)(2,1)}, u32[]{:S(2)}) copy-start(bf16[128,1024]{1,0:T(8,128)(2,1)} %param.11) | copy-start | bytes 786436
  9.6 159.6 %all-to-all-start = ((bf16[16,128,768]{2,1,0:T(8,128)(2,1)}), bf16[16,128,768]{2,1,0:T(8,128)(2,1)}, u32[]{:S(2)}, u32[]{:S(2)}) async-start(bf16[16,128,768]{2,1,0:T(8,128)(2,1)} %stack.2), calls=%async_computation | async-start | bytes 6291456 | tf_op jit(solution)/shard_map/all_to_all | solution.py:17
  28.2 218.4 %all-gather.4.cloned.1.call-start = ((), (), s32[]{:S(2)}) async-start(), calls=%async_computation.1 | async-start | bytes 6488064 | tf_op jit(solution)/shard_map/all_gather | solution.py:50
  172.9 5.6 %copy-start.9 = (f32[32,256]{1,0:T(8,128)S(1)}, f32[32,256]{1,0:T(8,128)}, u32[]{:S(2)}) copy-start(f32[32,256]{1,0:T(8,128)} %param.17) | copy-start | bytes 98308
  172.9 5.7 %copy-start.10 = (s32[128]{0:T(128)S(1)}, s32[128]{0:T(128)}, u32[]{:S(2)}) copy-start(s32[128]{0:T(128)} %param.14) | copy-start | bytes 1540
  176.1 142.2 %all-gather.6.cloned.1.call-start = ((), (), s32[]{:S(2)}) async-start(), calls=%async_computation.2 | async-start | bytes 6488064 | tf_op jit(solution)/shard_map/all_gather | solution.py:51
  318.3 3.3 copy-start.7
  325.4 4.5 copy-start.2
  331.8 1.3 copy-start.4
  331.8 1.3 copy-start.1
  333.1 1.3 copy-start.5
  333.1 1.3 copy-start.8
  334.4 3.3 copy-start.7
  341.5 4.5 copy-start.2
  347.9 1.3 copy-start.4
  347.9 1.3 copy-start.1
  349.2 1.3 copy-start.5
  349.3 1.3 copy-start.8
  350.5 3.3 copy-start.7
  357.7 4.5 copy-start.2
  364.0 1.3 copy-start.4
  364.1 1.3 copy-start.1
  365.4 1.3 copy-start.5
  365.4 1.3 copy-start.8
  366.7 3.3 copy-start.7
  373.8 4.5 copy-start.2
  380.2 1.3 copy-start.4
  380.2 1.3 copy-start.1
  381.5 1.3 copy-start.5
  381.5 1.3 copy-start.8
  382.8 3.3 copy-start.7
  389.9 4.5 copy-start.2
  396.3 1.3 copy-start.4
  396.3 1.3 copy-start.1
  397.6 1.3 copy-start.5
  397.6 1.3 copy-start.8
  398.9 3.3 copy-start.7
  406.0 4.5 copy-start.2
  412.4 1.3 copy-start.4
  412.4 1.3 copy-start.1
  413.7 1.3 copy-start.5
  413.8 1.3 copy-start.8
  415.0 3.3 copy-start.7
  422.2 4.5 copy-start.2
  428.5 1.3 copy-start.4
  428.6 1.3 copy-start.1
  429.9 1.3 copy-start.5
  429.9 1.3 copy-start.8
  431.2 3.3 copy-start.7
  438.3 4.5 copy-start.2
  444.7 1.3 copy-start.4
  444.7 1.3 copy-start.1
  446.0 1.3 copy-start.5
  446.0 1.3 copy-start.8
Sparse Core Ops, SparseCore 0:
  176.2 70.2 all-gather.3
  248.7 69.5 all-gather.5
